TPU v7x, 256 devices: a whole 4x4x8 slice. The times are simulated.
256 devices in a mesh: dp: 16 (over z, y_hi), row: 4 (over y_lo, core), col: 4 (over x).
Axes of the slice: x: 4, y: 4 (y_hi: 2, y_lo: 2; y = y_hi * 2 + y_lo), z: 8, core: 2. Of those that a mesh axis runs over, the one named last changes fastest.
Arguments:
- tokens: bfloat16 [7168, 4096], P(('dp', 'col'), 'row'), may hold values from -6 to 6
- gate_up: bfloat16 [2, 4096, 14336], P(None, 'row', ('dp', 'col')), may hold values from -0.09375 to 0.09375
- down_weight: bfloat16 [14336, 4096], P(('dp', 'col'), 'row'), may hold values from -0.046875 to 0.046875
Outputs:
- mixed: bfloat16 [7168, 4096], P(('dp', 'col'), 'row')
- col_check: float32 [4096], P('row')
- row_check: float32 [7168], P(('dp', 'col'))
All inputs are finite; a program needn't handle non-finite values.
Results may differ from a plain program's by a relative error of at most 0.0049.
Values may be sent and summed in bfloat16 or wider, within the bound.
No kernel may reach another device: no remote copies, remote signals or barrier semaphores. Data moves between devices by JAX's collectives and lax.ppermute only.
A program may use at most 128 MiB of HBM per device.

v0:
```python
import math
import jax
import jax.numpy as jnp
from jax import lax
from jax.sharding import PartitionSpec as P


def swiglu(partial_value):
    return (jax.nn.silu(partial_value[:, 0]) * partial_value[:, 1]).astype(jnp.bfloat16)


def hidden_units(partial_value):
    share = lax.psum_scatter(partial_value, "row", scatter_dimension=0, tiled=True)
    return lax.all_gather(swiglu(share), "row", axis=0, tiled=True)


def make_accumulate(hidden, shard_piece):
    columns_wide = hidden.astype(jnp.float32)
    piece_wide = shard_piece.astype(jnp.float32)
    output_part = jnp.dot(hidden, shard_piece, preferred_element_type=jnp.float32)
    column_part = jnp.dot(
        jnp.sum(columns_wide, axis=0), piece_wide, precision=lax.Precision.HIGHEST
    )
    row_part = jnp.dot(columns_wide, jnp.sum(piece_wide, axis=1), precision=lax.Precision.HIGHEST)
    return (output_part, column_part, row_part)


def per_device(tokens, gate_up, down_weight):
    total_tokens = tokens.shape[0] * lax.axis_size(("dp", "col"))
    model_width = tokens.shape[1] * lax.axis_size("row")
    group_rows = lax.all_gather(tokens, "col", axis=0, tiled=True)
    partial_value = jnp.einsum(
        "td,gdf->tgf",
        group_rows,
        lax.all_gather(gate_up, "dp", axis=2, tiled=True),
        preferred_element_type=jnp.float32,
    )
    hidden = hidden_units(partial_value)
    output_part, column_part, row_part = make_accumulate(
        hidden, lax.all_gather(down_weight, "dp", axis=0, tiled=True)
    )
    mixed, row_share = (
        lax.psum_scatter(output_part, "col", scatter_dimension=0, tiled=True),
        lax.psum_scatter(row_part, "col", scatter_dimension=0, tiled=True),
    )
    col_check = lax.psum(column_part, ("dp", "col")) / math.sqrt(total_tokens)
    row_check = lax.psum(row_share, "row") / math.sqrt(model_width)
    return (mixed.astype(jnp.bfloat16), col_check, row_check)


def solution(mesh):
    placed = (P(("dp", "col"), "row"), P(None, "row", ("dp", "col")), P(("dp", "col"), "row"))
    return jax.shard_map(
        per_device,
        mesh=mesh,
        in_specs=placed,
        out_specs=(P(("dp", "col"), "row"), P("row"), P(("dp", "col"))),
        check_vma=False,
    )
```

profile of v0, /device:TPU:8, one launch (start us, length us, event | category | flops | bytes accessed | tf_op | source)
XLA Modules:
  0.0 748.7 jit_solution(9035475301600994231)
XLA Ops:
  7.2 0.0 all-gather.4.cloned.1.call-start
  7.2 0.7 all-gather.4.cloned.1.call-update
  7.9 0.0 reduce-scatter.3.cloned.1.call-start
  7.9 14.2 %all_gather.12 = bf16[448,1024]{1,0:T(8,128)(2,1)S(1)} all-gather(bf16[112,1024]{1,0:T(8,128)(2,1)} %param.3), channel_id=1, replica_groups=mesh['dp'=16,'row'=4,'col'=4] {'col'}, dimensions={0}, use_global_device_ids=true | all-gather | bytes 1146880 | tf_op jit(solution)/shard_map/all_gather | solution.py:31
  22.2 192.1 %all-gather.4.cloned.1.call-done = bf16[2,1024,3584]{1,2,0:T(8,128)(2,1)} async-done(((bf16[2,1024,224]{1,2,0:T(8,128)(2,1)}), bf16[2,1024,3584]{1,2,0:T(8,128)(2,1)}) %all-gather.4.cloned.1.call-update) | async-done | bytes 14680080 | tf_op jit(solution)/shard_map/all_gather | solution.py:35
  214.2 22.2 %fusion.2 = f32[448,2,3584]{2,0,1:T(8,128)} fusion(bf16[2,1024,3584]{1,2,0:T(8,128)(2,1)} %all-gather.4.cloned.1.call-done, bf16[448,1024]{1,0:T(8,128)(2,1)S(1)} %all_gather.12), kind=kOutput, calls=%fused_computation.6 | convolution fusion | flops 6576668672 | bytes 28442624 | tf_op jit(solution)/shard_map/td,gdf->tgf/dot_general | solution.py:32
  236.5 0.0 reduce-scatter.3.cloned.1.call-update
  236.5 0.0 all-gather.8.cloned.1.call-start
  236.5 0.7 all-gather.8.cloned.1.call-update
  237.2 0.0 all-gather.6.cloned.1.call-start
  237.3 113.1 %reduce-scatter.3.cloned.1.call-done = f32[112,2,3584]{2,0,1:T(8,128)} async-done(((f32[448,2,3584]{2,0,1:T(8,128)}), f32[112,2,3584]{2,0,1:T(8,128)}) %reduce-scatter.3.cloned.1.call-update) | async-done | bytes 3211280 | tf_op jit(solution)/shard_map/reduce_scatter | solution.py:13
  350.3 3.2 fusion.1
  353.6 0.0 all-gather.6.cloned.1.call-update
  353.6 0.0 copy-start.1
  353.6 0.0 reduce-scatter.5.cloned.1.call-start
  353.6 126.6 %all-gather.8.cloned.1.call-done = bf16[3584,1024]{1,0:T(8,128)(2,1)} async-done(((bf16[224,1024]{1,0:T(8,128)(2,1)}), bf16[3584,1024]{1,0:T(8,128)(2,1)}) %all-gather.8.cloned.1.call-update) | async-done | bytes 7340048 | tf_op jit(solution)/shard_map/all_gather | solution.py:40
  480.3 38.6 %all-gather.6.cloned.1.call-done = bf16[448,3584]{1,0:T(8,128)(2,1)} async-done(((bf16[112,3584]{1,0:T(8,128)(2,1)}), bf16[448,3584]{1,0:T(8,128)(2,1)}) %all-gather.6.cloned.1.call-update) | async-done | bytes 3211280 | tf_op jit(solution)/shard_map/all_gather | solution.py:14
  518.8 8.8 %fusion.4 = f32[448,1024]{1,0:T(8,128)} fusion(bf16[448,3584]{1,0:T(8,128)(2,1)} %all-gather.6.cloned.1.call-done, bf16[3584,1024]{1,0:T(8,128)(2,1)} %all-gather.8.cloned.1.call-done), kind=kOutput, calls=%fused_computation.10 | convolution fusion | flops 3288334336 | bytes 12386304 | tf_op jit(solution)/shard_map/dot_general | solution.py:20
  527.6 0.0 reduce-scatter.5.cloned.1.call-update
  527.6 0.0 copy-done.1
  527.6 0.6 dynamic-slice
  528.9 0.0 copy-start
  528.9 4.3 convert_reduce_fusion
  533.2 0.0 copy-done
  533.2 0.6 convert_reduce_fusion.1
  533.8 2.6 fusion.6
  536.4 10.9 %all-reduce = f32[448]{0:T(512)S(1)} all-reduce(f32[448]{0:T(512)S(1)} %bitcast.24), channel_id=4, replica_groups=mesh['dp'=16,'row'=4,'col'=4] {'col'}, use_global_device_ids=true, to_apply=%region_5.6.clone | all-reduce | flops 448 | bytes 3584
  547.2 0.1 dynamic-slice.1
  547.3 6.5 psum.15
  553.8 5.2 fusion.5
  559.0 180.3 %psum.14 = f32[1024]{0:T(1024)S(1)} all-reduce(f32[1024]{0:T(1024)S(1)} %bitcast.23), channel_id=1, replica_groups=mesh['dp'=16,'row'=4,'col'=4] {'dp','col'}, use_global_device_ids=true, to_apply=%region_3.4 | all-reduce | flops 1024 | bytes 8192 | tf_op jit(solution)/shard_map/psum | solution.py:46
  739.3 0.5 broadcast_multiply_fusion.1
  739.8 0.6 broadcast_multiply_fusion
  740.4 0.0 reduce-scatter.5.cloned.1.call-done
  740.4 1.7 convert_element_type.13
  (2 shorter events, 0.0 us)
Async XLA Ops:
  7.2 207.1 %all-gather.4.cloned.1.call-start = ((), (), s32[]{:S(2)}) async-start(), calls=%async_computation.2 | async-start | bytes 15597568 | tf_op jit(solution)/shard_map/all_gather | solution.py:35
  7.9 342.4 %reduce-scatter.3.cloned.1.call-start = ((), (), s32[]{:S(2)}) async-start(), calls=%async_computation.3 | async-start | bytes 16056320 | tf_op jit(solution)/shard_map/reduce_scatter | solution.py:13
  236.5 243.8 %all-gather.8.cloned.1.call-start = ((), (), s32[]{:S(2)}) async-start(), calls=%async_computation.5 | async-start | bytes 7798784 | tf_op jit(solution)/shard_map/all_gather | solution.py:40
  237.2 281.6 %all-gather.6.cloned.1.call-start = ((), (), s32[]{:S(2)}) async-start(), calls=%async_computation.4 | async-start | bytes 4014080 | tf_op jit(solution)/shard_map/all_gather | solution.py:14
  353.6 174.1 %copy-start.1 = (u32[256]{0:T(256)S(1)}, u32[256]{0:T(256)}, u32[]{:S(2)}) copy-start(u32[256]{0:T(256)} %constant.16) | copy-start | bytes 3076
  353.6 386.8 %reduce-scatter.5.cloned.1.call-start = ((), (), s32[]{:S(2)}) async-start(), calls=%async_computation.6 | async-start | bytes 2293760 | tf_op jit(solution)/shard_map/reduce_scatter | solution.py:43
  528.9 4.3 copy-start
Sparse Core Ops, SparseCore 0:
  10.6 203.5 all-gather.3
  236.6 113.6 reduce-scatter.2
  352.9 127.3 all-gather.7
  481.9 36.8 all-gather.5
  527.7 32.7 reduce-scatter.4
where the time goes:
time: 749 us
  waiting for transfers between devices  472 us (63%)
  blocking collectives  212 us (28%)
  matrix products  38.7 us (5%)
  between operations  14.5 us (2%)
  other arithmetic  10.9 us (1%)
    all_gather x1, waiting for transfers between devices, per_device(): lax.all_gather(gate_up, 'dp', axis=2, tiled=True)  192 us
    psum x1, blocking collectives, per_device(): col_check = lax.psum(column_part, ('dp', 'col')) / math.sqrt(total_tokens)  180 us
    all_gather x1, waiting for transfers between devices, per_device(): lax.all_gather(down_weight, 'dp', axis=0, tiled=True)  127 us
    reduce_scatter x1, waiting for transfers between devices, hidden_units(): lax.psum_scatter(partial_value, 'row', scatter_dimension=0, tiled=True)  113 us
    all_gather x1, waiting for transfers between devices, hidden_units(): return lax.all_gather(swiglu(share), 'row', axis=0, tiled=True)  38.6 us
    dot_general x1, matrix products, per_device(): jnp.einsum('td,gdf->tgf', group_rows, lax.all_gather(gate_up, 'dp', axis=...  22.2 us
  transfers between devices with their start and end apart: 5, of which 4 were waited for; matrix products, arithmetic and copies ran while one was open for 2% of the time, Pallas kernels for 0%

commit v1 on v0

--- a/solution.py
+++ b/solution.py
@@ -43,7 +43,7 @@
         lax.psum_scatter(output_part, "col", scatter_dimension=0, tiled=True),
         lax.psum_scatter(row_part, "col", scatter_dimension=0, tiled=True),
     )
-    col_check = lax.psum(column_part, ("dp", "col")) / math.sqrt(total_tokens)
+    col_check = lax.psum(lax.psum(column_part, "dp"), "col") / math.sqrt(total_tokens)
     row_check = lax.psum(row_share, "row") / math.sqrt(model_width)
     return (mixed.astype(jnp.bfloat16), col_check, row_check)
 

time: 749 us -> 610 us (0.81)
  blocking collectives: 212 us -> 72.6 us
    psum x1 -> x2, blocking collectives: 180 us -> 52.7 us  [the longest x1 42.2 us: per_device(): lax.psum(column_part, 'dp')]
    unnamed x1 -> x0, blocking collectives: 10.9 us -> none
  transfers between devices with their start and end apart: 5 -> 5, of which waited for: 4 -> 4; matrix products, arithmetic and copies ran while one was open for 2% -> 3% of each run, Pallas kernels for 0% -> 0%
where the time goes in v1:
time: 610 us; the launch traced here: 608 us
  waiting for transfers between devices  472 us (77%)
  blocking collectives  72.6 us (12%)
  matrix products  36.5 us (6%)
  between operations  14.8 us (2%)
  other arithmetic  10.9 us (2%)
    all_gather x1, waiting for transfers between devices, per_device(): lax.all_gather(gate_up, 'dp', axis=2, tiled=True)  192 us
    all_gather x1, waiting for transfers between devices, per_device(): lax.all_gather(down_weight, 'dp', axis=0, tiled=True)  127 us
    reduce_scatter x1, waiting for transfers between devices, hidden_units(): lax.psum_scatter(partial_value, 'row', scatter_dimension=0, tiled=True)  113 us
    psum x1, blocking collectives, per_device(): lax.psum(column_part, 'dp')  42.2 us
    all_gather x1, waiting for transfers between devices, hidden_units(): return lax.all_gather(swiglu(share), 'row', axis=0, tiled=True)  38.6 us
    dot_general x1, matrix products, per_device(): jnp.einsum('td,gdf->tgf', group_rows, lax.all_gather(gate_up, 'dp', axis=...  22.2 us
    all_gather x1, blocking collectives, per_device(): group_rows = lax.all_gather(tokens, 'col', axis=0, tiled=True)  14.2 us
  transfers between devices with their start and end apart: 5, of which 4 were waited for; matrix products, arithmetic and copies ran while one was open for 3% of the time, Pallas kernels for 0%

profile of v1, /device:TPU:8, one launch (start us, length us, event | category | flops | bytes accessed | tf_op | source)
XLA Modules:
  0.0 607.8 jit_solution(11758015143369375772)
XLA Ops:
  7.2 0.0 all-gather.4.cloned.1.call-start
  7.2 0.7 all-gather.4.cloned.1.call-update
  7.9 0.0 reduce-scatter.3.cloned.1.call-start
  7.9 14.2 %all_gather.12 = bf16[448,1024]{1,0:T(8,128)(2,1)S(1)} all-gather(bf16[112,1024]{1,0:T(8,128)(2,1)} %param.3), channel_id=1, replica_groups=mesh['dp'=16,'row'=4,'col'=4] {'col'}, dimensions={0}, use_global_device_ids=true | all-gather | bytes 1146880 | tf_op jit(solution)/shard_map/all_gather | solution.py:31
  22.2 192.1 %all-gather.4.cloned.1.call-done = bf16[2,1024,3584]{1,2,0:T(8,128)(2,1)} async-done(((bf16[2,1024,224]{1,2,0:T(8,128)(2,1)}), bf16[2,1024,3584]{1,2,0:T(8,128)(2,1)}) %all-gather.4.cloned.1.call-update) | async-done | bytes 14680080 | tf_op jit(solution)/shard_map/all_gather | solution.py:35
  214.2 22.2 %fusion.2 = f32[448,2,3584]{2,0,1:T(8,128)} fusion(bf16[2,1024,3584]{1,2,0:T(8,128)(2,1)} %all-gather.4.cloned.1.call-done, bf16[448,1024]{1,0:T(8,128)(2,1)S(1)} %all_gather.12), kind=kOutput, calls=%fused_computation.6 | convolution fusion | flops 6576668672 | bytes 28442624 | tf_op jit(solution)/shard_map/td,gdf->tgf/dot_general | solution.py:32
  236.5 0.0 reduce-scatter.3.cloned.1.call-update
  236.5 0.0 all-gather.8.cloned.1.call-start
  236.5 0.7 all-gather.8.cloned.1.call-update
  237.2 0.0 all-gather.6.cloned.1.call-start
  237.3 113.1 %reduce-scatter.3.cloned.1.call-done = f32[112,2,3584]{2,0,1:T(8,128)} async-done(((f32[448,2,3584]{2,0,1:T(8,128)}), f32[112,2,3584]{2,0,1:T(8,128)}) %reduce-scatter.3.cloned.1.call-update) | async-done | bytes 3211280 | tf_op jit(solution)/shard_map/reduce_scatter | solution.py:13
  350.3 3.2 fusion.1
  353.6 0.0 all-gather.6.cloned.1.call-update
  353.6 0.0 copy-start.2
  353.6 0.0 reduce-scatter.5.cloned.1.call-start
  353.6 126.6 %all-gather.8.cloned.1.call-done = bf16[3584,1024]{1,0:T(8,128)(2,1)} async-done(((bf16[224,1024]{1,0:T(8,128)(2,1)}), bf16[3584,1024]{1,0:T(8,128)(2,1)}) %all-gather.8.cloned.1.call-update) | async-done | bytes 7340048 | tf_op jit(solution)/shard_map/all_gather | solution.py:40
  480.3 38.6 %all-gather.6.cloned.1.call-done = bf16[448,3584]{1,0:T(8,128)(2,1)} async-done(((bf16[112,3584]{1,0:T(8,128)(2,1)}), bf16[448,3584]{1,0:T(8,128)(2,1)}) %all-gather.6.cloned.1.call-update) | async-done | bytes 3211280 | tf_op jit(solution)/shard_map/all_gather | solution.py:14
  518.8 8.8 %fusion.4 = f32[448,1024]{1,0:T(8,128)} fusion(bf16[448,3584]{1,0:T(8,128)(2,1)} %all-gather.6.cloned.1.call-done, bf16[3584,1024]{1,0:T(8,128)(2,1)} %all-gather.8.cloned.1.call-done), kind=kOutput, calls=%fused_computation.10 | convolution fusion | flops 3288334336 | bytes 12386304 | tf_op jit(solution)/shard_map/dot_general | solution.py:20
  527.6 0.0 copy-start.1
  527.6 0.0 reduce-scatter.5.cloned.1.call-update
  527.6 0.0 copy-done.2
  527.6 0.6 dynamic-slice
  529.2 0.0 copy-start
  529.2 4.3 convert_reduce_fusion
  533.5 0.0 copy-done.1
  533.5 0.6 convert_reduce_fusion.1
  534.1 0.3 copy-done
  534.4 2.9 fusion.5
  537.4 42.2 %psum.21 = f32[1024]{0:T(1024)S(1)} all-reduce(f32[1024]{0:T(1024)S(1)} %bitcast.23), channel_id=1, replica_groups=mesh['dp'=16,'row'=4,'col'=4] {'dp'}, use_global_device_ids=true, to_apply=%region_3.4 | all-reduce | flops 1024 | bytes 8192 | tf_op jit(solution)/shard_map/psum | solution.py:46
  579.6 2.6 fusion.6
  582.1 10.5 %all-reduce.1 = (f32[1024]{0:T(1024)S(1)}, f32[448]{0:T(512)S(1)}) all-reduce(f32[1024]{0:T(1024)S(1)} %psum.21, f32[448]{0:T(512)S(1)} %bitcast.24), channel_id=1, replica_groups=mesh['dp'=16,'row'=4,'col'=4] {'col'}, use_global_device_ids=true, to_apply=%region_4.5 | all-reduce | flops 1472 | bytes 11776 | tf_op jit(solution)/shard_map/psum | solution.py:46
  592.7 0.1 dynamic-slice.1
  592.7 5.6 psum.23
  598.4 0.5 broadcast_multiply_fusion.1
  598.9 0.6 broadcast_multiply_fusion
  599.5 0.0 reduce-scatter.5.cloned.1.call-done
  599.5 1.7 convert_element_type.13
  (2 shorter events, 0.0 us)
Async XLA Ops:
  7.2 207.1 %all-gather.4.cloned.1.call-start = ((), (), s32[]{:S(2)}) async-start(), calls=%async_computation.2 | async-start | bytes 15597568 | tf_op jit(solution)/shard_map/all_gather | solution.py:35
  7.9 342.4 %reduce-scatter.3.cloned.1.call-start = ((), (), s32[]{:S(2)}) async-start(), calls=%async_computation.3 | async-start | bytes 16056320 | tf_op jit(solution)/shard_map/reduce_scatter | solution.py:13
  236.5 243.8 %all-gather.8.cloned.1.call-start = ((), (), s32[]{:S(2)}) async-start(), calls=%async_computation.5 | async-start | bytes 7798784 | tf_op jit(solution)/shard_map/all_gather | solution.py:40
  237.2 281.6 %all-gather.6.cloned.1.call-start = ((), (), s32[]{:S(2)}) async-start(), calls=%async_computation.4 | async-start | bytes 4014080 | tf_op jit(solution)/shard_map/all_gather | solution.py:14
  353.6 174.1 %copy-start.2 = (u32[256]{0:T(256)S(1)}, u32[256]{0:T(256)}, u32[]{:S(2)}) copy-start(u32[256]{0:T(256)} %constant.16) | copy-start | bytes 3076
  353.6 245.9 %reduce-scatter.5.cloned.1.call-start = ((), (), s32[]{:S(2)}) async-start(), calls=%async_computation.6 | async-start | bytes 2293760 | tf_op jit(solution)/shard_map/reduce_scatter | solution.py:43
  527.6 5.9 copy-start.1
  529.2 5.3 copy-start
Sparse Core Ops, SparseCore 0:
  10.6 203.5 all-gather.3
  236.6 113.6 reduce-scatter.2
  352.9 127.3 all-gather.7
  481.9 36.8 all-gather.5
  527.7 32.6 reduce-scatter.4
